TPU v7x, 256 devices: a whole 4x4x8 slice. The times are simulated.
256 devices in a mesh: dp: 4 (over x), expert: 64 (over z, y, core).
Axes of the slice: x: 4, y: 4, z: 8, core: 2. Of those that a mesh axis runs over, the one named last changes fastest.
Arguments:
- hidden_in: bfloat16 [32768, 2048], P(('dp', 'expert')), may hold values from -6 to 6
- queries: bfloat16 [32768, 2048], P(('dp', 'expert')), may hold values from -150 to 150, as said below
- keys_values: bfloat16 [32768, 512], P(('dp', 'expert')), may hold values from -5 to 5
- segment_ids: int32 [4, 8192], P('dp', 'expert'), may hold values from 0 to 7, never falling along the last dimension, each value on 1 to 4096 neighbouring positions
- routes: int32 [32768, 8], P(('dp', 'expert')), may hold values from 0 to 63, all different within a row; in each aligned block of 128 rows (0 to 127, 128 to 255, ...) at most 24 rows name the same one
- gate_weights: float32 [32768, 8], P(('dp', 'expert')), may hold values from 0.05 to 1
- page_table: int32 [4, 512], P('dp'), may hold values from 0 to 511, each once within a row
- out_weight: bfloat16 [2048, 2048], P('dp'), may hold values from -0.125 to 0.125
- norm_gain: float32 [2048], replicated, may hold values from 0.1 to 1.9
- expert_gate: bfloat16 [64, 2048, 384], P('expert'), may hold values from -0.125 to 0.125
- expert_up: bfloat16 [64, 2048, 384], P('expert'), may hold values from -0.125 to 0.125
- expert_down: bfloat16 [64, 384, 2048], P('expert'), may hold values from -0.3125 to 0.3125
Outputs:
- hidden_out: bfloat16 [32768, 2048], P(('dp', 'expert'))
- cache_pages: bfloat16 [2048, 16, 512], P(('dp', 'expert'))
Inputs may be any that keep to these rules, and one draw needn't show every extreme that they name: `queries`: queries (hidden draw: some equal a multiple of their own key). `segment_ids`: within a pack numbers never fall; each prompt has 1 to 4096 tokens and some prompt has exactly 4096. `routes`: each row names 8 different experts; among the rows of one device no expert is named more than 24 times, a bound that some block reaches. `page_table`: each row is a permutation of its pack's 512 slots.
All inputs are finite; a program needn't handle non-finite values.
Results may differ from a plain program's by a relative error of at most 0.007.
Values may be sent and summed in bfloat16 or wider, within the bound.
A program may use at most 128 MiB of HBM per device.

v0:
```python
import math

import jax
import jax.numpy as jnp
from jax import lax
from jax.sharding import PartitionSpec as P

HD = 128
HQ = 16
HK = 2
TOP = 8
PAGE = 16


neg_big = -1e30
norm_eps = 1e-06


def body(
    hidden_in,
    queries,
    keys_values,
    segment_ids,
    routes,
    gate_weights,
    page_table,
    out_weight,
    norm_gain,
    expert_gate,
    expert_up,
    expert_down,
):
    tok_rows = hidden_in.shape[0]
    width = hidden_in.shape[1]
    groups = HQ // HK
    kv_width = HK * HD
    member = lax.axis_index("expert")
    first_row = member * tok_rows
    query_blocks = queries.reshape(tok_rows, HK, groups, HD)
    seg_local = segment_ids.reshape(tok_rows)
    query_pos = first_row + jnp.arange(tok_rows, dtype=jnp.int32)
    last_pos = first_row + tok_rows - 1
    slot_count = tok_rows // PAGE
    table_row = page_table.reshape(-1)
    pages_total = table_row.shape[0]
    targets = member * slot_count + jnp.arange(slot_count, dtype=jnp.int32)
    matches = (table_row[None, :] == targets[:, None]).astype(jnp.int32)
    page_of_slot = jnp.sum(matches * jnp.arange(pages_total, dtype=jnp.int32)[None, :], axis=1)
    score_scale = 1.0 / math.sqrt(HD)

    def attend_block(carried, inputs):
        running_max, running_sum, running_acc = carried
        kv_block, seg_block, block_start = inputs
        row_count = kv_block.shape[0]
        key_part = kv_block[:, :kv_width].reshape(row_count, HK, HD)
        value_part = kv_block[:, kv_width:].reshape(row_count, HK, HD)
        key_pos = block_start + jnp.arange(row_count, dtype=jnp.int32)
        allowed = (key_pos[None, :] <= query_pos[:, None]) & (
            seg_block[None, :] == seg_local[:, None]
        )
        allowed_wide = allowed[:, None, None, :]
        scores = (
            jnp.einsum("thgd,shd->thgs", query_blocks, key_part, preferred_element_type=jnp.float32)
            * score_scale
        )
        masked = jnp.where(allowed_wide, scores, neg_big)
        new_max = jnp.maximum(running_max, jnp.max(masked, axis=3))
        probabilities = jnp.where(allowed_wide, jnp.exp(masked - new_max[..., None]), 0.0)
        factor = jnp.exp(running_max - new_max)
        new_sum = running_sum * factor + jnp.sum(probabilities, axis=3)
        weighted = jnp.einsum(
            "thgs,shd->thgd",
            probabilities.astype(jnp.bfloat16),
            value_part,
            preferred_element_type=jnp.float32,
        )
        new_acc = running_acc * factor[..., None] + weighted
        return (new_max, new_sum, new_acc)

    def keep_state(carried, inputs):
        return carried

    def advance(carried, inputs):
        kv_block, seg_block, block_start = inputs
        row_count = kv_block.shape[0]
        needed = block_start <= last_pos
        return (lax.cond(needed, attend_block, keep_state, carried, inputs), None)

    start_state = (
        jnp.full((tok_rows, HK, groups), neg_big, jnp.float32),
        jnp.zeros((tok_rows, HK, groups), jnp.float32),
        jnp.zeros((tok_rows, HK, groups, HD), jnp.float32),
    )
    start_cache = jnp.zeros((slot_count, PAGE, keys_values.shape[1]), jnp.bfloat16)
    softmax_state = start_state
    cache_slots = start_cache
    kv_piece = lax.all_gather(keys_values, "expert", axis=0, tiled=True)
    seg_piece = lax.all_gather(seg_local, "expert", axis=0, tiled=True)
    piece_rows = kv_piece.shape[0]
    block_rows = math.gcd(piece_rows, 512)
    block_count = piece_rows // block_rows
    kv_steps = kv_piece.reshape(block_count, block_rows, kv_piece.shape[1])
    seg_steps = seg_piece.reshape(block_count, block_rows)
    block_starts = block_rows * jnp.arange(block_count, dtype=jnp.int32)
    softmax_state, _ = lax.scan(advance, softmax_state, (kv_steps, seg_steps, block_starts))
    local_row = page_of_slot * PAGE
    inside = (local_row >= 0) & (local_row < piece_rows)
    safe_row = jnp.clip(local_row, 0, piece_rows - PAGE)

    def take_page(row_start):
        return lax.dynamic_slice_in_dim(kv_piece, row_start, PAGE, 0)

    page_rows = jax.vmap(take_page)(safe_row)
    cache_slots = jnp.where(inside[:, None, None], page_rows, cache_slots)
    final_state, cache_slots = (softmax_state, cache_slots)
    running_max, running_sum, running_acc = final_state
    attended = (
        (running_acc / running_sum[..., None]).reshape(tok_rows, HQ * HD).astype(jnp.bfloat16)
    )
    projected = jnp.dot(
        attended,
        lax.all_gather(out_weight, "dp", axis=0, tiled=True),
        preferred_element_type=jnp.float32,
    )
    residual = hidden_in.astype(jnp.float32) + projected
    normed = (
        residual
        * lax.rsqrt(jnp.mean(residual * residual, axis=1, keepdims=True) + norm_eps)
        * norm_gain
    ).astype(jnp.bfloat16)
    experts_total = lax.axis_size("expert")
    capacity = min(tok_rows, (3 * tok_rows * TOP + 2 * experts_total - 1) // (2 * experts_total))
    flat_routes = routes.reshape(-1)
    one_hot = (flat_routes[:, None] == jnp.arange(experts_total, dtype=jnp.int32)[None, :]).astype(
        jnp.int32
    )
    before = jnp.cumsum(one_hot, axis=0) - one_hot
    slot_rank = jnp.sum(before * one_hot, axis=1)
    target_rows = flat_routes * capacity + slot_rank
    outgoing = (
        jnp.zeros((experts_total * capacity, width), jnp.bfloat16)
        .at[target_rows]
        .set(jnp.repeat(normed, TOP, axis=0))
    )
    outgoing = outgoing.reshape(experts_total, capacity, width)
    arrived_rows = lax.all_to_all(outgoing, "expert", split_axis=0, concat_axis=0, tiled=True)
    senders = arrived_rows.shape[0]
    slot_total = arrived_rows.shape[1]
    flat_rows = arrived_rows.reshape(senders * slot_total, width)
    gate_value = jnp.dot(flat_rows, expert_gate[0], preferred_element_type=jnp.float32)
    up_value = jnp.dot(flat_rows, expert_up[0], preferred_element_type=jnp.float32)
    hidden_units = (jax.nn.silu(gate_value) * up_value).astype(jnp.bfloat16)
    result = jnp.dot(hidden_units, expert_down[0], preferred_element_type=jnp.float32).astype(
        jnp.bfloat16
    )
    returned = lax.all_to_all(
        result.reshape(senders, slot_total, width),
        "expert",
        split_axis=0,
        concat_axis=0,
        tiled=True,
    )
    picked = returned.reshape(experts_total * capacity, width)[target_rows].reshape(
        tok_rows, TOP, width
    )
    shares = gate_weights / jnp.sum(gate_weights, axis=1, keepdims=True)
    combined = jnp.einsum("tk,tkd->td", shares, picked.astype(jnp.float32))
    hidden_out = (residual + combined).astype(jnp.bfloat16)
    return (hidden_out, cache_slots)


def solution(mesh):
    return jax.shard_map(
        body,
        mesh=mesh,
        in_specs=(
            P(("dp", "expert"), None),
            P(("dp", "expert"), None),
            P(("dp", "expert"), None),
            P("dp", "expert"),
            P(("dp", "expert"), None),
            P(("dp", "expert"), None),
            P("dp", None),
            P("dp", None),
            P(),
            P("expert", None, None),
            P("expert", None, None),
            P("expert", None, None),
        ),
        out_specs=(P(("dp", "expert"), None), P(("dp", "expert"), None, None)),
        check_vma=False,
    )
```

profile of v0, /device:TPU:1, one launch (start us, length us, event | category | flops | bytes accessed | tf_op | source)
XLA Modules:
  0.0 573.1 jit_solution(1205731192208874097)
XLA Ops:
  11.3 44.2 %all-gather = s32[1,8192]{1,0:T(1,128)S(1)} all-gather(s32[1,128]{1,0:T(1,128)S(1)} %copy-done.2), channel_id=2, replica_groups=mesh['dp'=4,'expert'=64] {'expert'}, dimensions={1}, use_global_device_ids=true | all-gather | bytes 33280 | tf_op jit(solution)/shard_map/all_gather | solution.py:98
  56.7 18.0 %reduce-window.6 = s32[64,8,128]{2,1,0:T(8,128)S(1)} reduce-window(s32[64,8,128]{2,1,0:T(8,128)S(1)} %fusion.34, s32[]{:T(128)} %copy.87), window={size=1x1x128 pad=0_0x0_0x127_0}, to_apply=%region_7.8 | reduce-window | flops 8323072 | bytes 524292 | tf_op jit(solution)/shard_map/reduce-window
  75.6 22.5 %all-gather.4.cloned.1.call-done = bf16[8192,512]{1,0:T(8,128)(2,1)} async-done(((bf16[128,512]{1,0:T(8,128)(2,1)}), bf16[8192,512]{1,0:T(8,128)(2,1)}) %all-gather.4.cloned.1.call-update) | async-done | bytes 8388624 | tf_op jit(solution)/shard_map/all_gather | solution.py:97
  98.1 12.3 %copy.42 = bf16[16,512,512]{1,2,0:T(8,128)(2,1)} copy(bf16[16,512,512]{2,1,0:T(8,128)(2,1)} %bitcast.109) | data formatting | bytes 16777216
  110.6 26.3 %while.19 = (s32[]{:T(128)}, f32[128,2,8]{0,2,1:T(8,128)S(1)}, f32[128,2,8]{0,2,1:T(8,128)S(1)}, f32[128,2,8,128]{3,0,2,1:T(8,128)S(1)}, s32[16]{0:T(128)S(1)}, ...) while((s32[]{:T(128)}, f32[128,2,8]{0,2,1:T(8,128)S(1)}, ...), condition=%wide.region_5.6_spmd.clone.clone, body=%wide.region_0.5_spmd.clone.sunk.clone | while | flops 551228032 | bytes 18232104 | solution.py:105
  111.9 5.7 conditional.4
  115.8 1.7 fusion.11
  139.6 42.9 %all-gather.6.cloned.1.call-done = bf16[2048,2048]{1,0:T(8,128)(2,1)} async-done(((bf16[512,2048]{1,0:T(8,128)(2,1)}), bf16[2048,2048]{1,0:T(8,128)(2,1)}) %all-gather.6.cloned.1.call-update) | async-done | bytes 8388624 | tf_op jit(solution)/shard_map/all_gather | solution.py:122
  182.5 4.8 multiply_reduce_fusion
  187.5 10.3 %scatter_custom_fusion = bf16[1536,2048]{1,0:T(8,128)(2,1)} fusion(s32[1024]{0:T(1024)S(1)} %bitcast.121, bf16[]{:T(256)} %constant.72.clone.1, bf16[128,2048]{1,0:T(8,128)(2,1)S(1)} %multiply_convert_fusion), kind=kCustom, calls=%fused_computation.27 | custom fusion | bytes 6815746 | tf_op jit(solution)/shard_map/scatter | solution.py:143
  197.7 186.5 %all_to_all.10 = bf16[64,24,2048]{2,1,0:T(8,128)(2,1)S(1)} all-to-all(bf16[64,24,2048]{2,1,0:T(8,128)(2,1)} %bitcast.108), channel_id=1, replica_groups=mesh['dp'=4,'expert'=64] {'expert'}, dimensions={0} | all-to-all | bytes 12582912 | tf_op jit(solution)/shard_map/all_to_all | solution.py:146
  384.2 2.6 copy-done.1
  386.8 4.9 fusion.26
  391.7 11.3 %convolution_convert_fusion = bf16[1536,2048]{1,0:T(8,128)(2,1)} fusion(bf16[1,384,2048]{2,1,0:T(8,128)(2,1)S(1)} %copy-done, bf16[1536,2048]{1,0:T(8,128)(2,1)} %bitcast.113, f32[1536,384]{1,0:T(8,128)} %fusion.26, bf16[1,2048,384]{2,1,0:T(8,128)(2,1)} %param.26), kind=kOutput, calls=%fused_computation.24 | convolution fusion | flops 4838522880 | bytes 18087936 | tf_op jit(solution)/shard_map/dot_general | solution.py:153
  403.1 7.4 %all-to-all-start.1 = ((bf16[64,24,2048]{2,1,0:T(8,128)(2,1)}), bf16[64,24,2048]{2,1,0:T(8,128)(2,1)}, u32[]{:S(2)}, u32[]{:S(2)}) async-start(bf16[64,24,2048]{2,1,0:T(8,128)(2,1)} %bitcast.111), calls=%async_computation.1 | async-start | bytes 12582912 | tf_op jit(solution)/shard_map/all_to_all | solution.py:156
  410.8 15.9 %while.18 = (s32[]{:T(128)}, bf16[8192,512]{1,0:T(8,128)(2,1)}, s32[8,2]{0,1:T(2,128)S(1)}, bf16[8,16,512]{2,1,0:T(8,128)(2,1)S(1)}) while((s32[]{:T(128)}, bf16[8192,512]{1,0:T(8,128)(2,1)}, s32[8,2]{0,1:T(2,128)S(1)}, bf16[8,16,512]{2,1,0:T(8,128)(2,1)S(1)}) %tuple.73), condition=%wide.while_cond.clone, body=%wide.while_body.sunk.clone | while | flops 2 | bytes 32857 | solution.py:111
  411.4 1.4 bitcast_dynamic-update-slice_fusion.3
  413.4 1.4 bitcast_dynamic-update-slice_fusion.3
  415.4 1.4 bitcast_dynamic-update-slice_fusion.3
  417.4 1.4 bitcast_dynamic-update-slice_fusion.3
  419.4 1.4 bitcast_dynamic-update-slice_fusion.3
  427.5 121.8 %all-to-all-done.1 = bf16[64,24,2048]{2,1,0:T(8,128)(2,1)} async-done(((bf16[64,24,2048]{2,1,0:T(8,128)(2,1)}), bf16[64,24,2048]{2,1,0:T(8,128)(2,1)}, u32[]{:S(2)}, u32[]{:S(2)}) %all-to-all-start.1) | async-done | bytes 6291488 | tf_op jit(solution)/shard_map/all_to_all | solution.py:156
  549.3 12.4 %gather_fusion = bf16[1024,2048]{1,0:T(8,128)(2,1)} fusion(bf16[1536,2048]{1,0:T(8,128)(2,1)} %bitcast.24, s32[1024]{0:T(1024)S(1)} %broadcast_clamp_fusion), kind=kCustom, calls=%fused_computation | custom fusion | bytes 8392704 | tf_op jit(solution)/shard_map/gather | solution.py:163
  561.7 3.4 fusion.17
  (136 shorter events, 34.0 us)
Async XLA Ops:
  7.2 384.5 %copy-start = (bf16[1,384,2048]{2,1,0:T(8,128)(2,1)S(1)}, bf16[1,384,2048]{2,1,0:T(8,128)(2,1)}, u32[]{:S(2)}) copy-start(bf16[1,384,2048]{2,1,0:T(8,128)(2,1)} %param.27) | copy-start | bytes 4718596
  7.2 68.0 %copy-start.3 = (s32[128,8]{0,1:T(8,128)S(1)}, s32[128,8]{0,1:T(8,128)}, u32[]{:S(2)}) copy-start(s32[128,8]{0,1:T(8,128)} %param.20) | copy-start | bytes 12292
  7.2 4.1 copy-start.2
  7.2 90.9 %all-gather.4.cloned.1.call-start = ((), (), s32[]{:S(2)}) async-start(), calls=%async_computation.2 | async-start | bytes 8519680 | tf_op jit(solution)/shard_map/all_gather | solution.py:97
  7.9 174.6 %all-gather.6.cloned.1.call-start = ((), (), s32[]{:S(2)}) async-start(), calls=%async_computation.3 | async-start | bytes 10485760 | tf_op jit(solution)/shard_map/all_gather | solution.py:122
  182.5 4.8 copy-start.5
  197.7 189.0 %copy-start.7 = (bf16[1,2048,384]{2,1,0:T(8,128)(2,1)S(1)}, bf16[1,2048,384]{2,1,0:T(8,128)(2,1)}, u32[]{:S(2)}) copy-start(bf16[1,2048,384]{2,1,0:T(8,128)(2,1)} %param.25) | copy-start | bytes 4718596
  384.2 2.6 copy-start.1
  403.0 7.4 %copy-start.4 = (f32[128,8]{0,1:T(8,128)S(1)}, f32[128,8]{0,1:T(8,128)}, u32[]{:S(2)}) copy-start(f32[128,8]{0,1:T(8,128)} %param.21) | copy-start | bytes 12292
  403.0 7.6 %copy-start.6 = (s32[1,512]{1,0:T(1,128)S(1)}, s32[1,512]{1,0:T(1,128)}, u32[]{:S(2)}) copy-start(s32[1,512]{1,0:T(1,128)} %param.22) | copy-start | bytes 6148
  403.1 146.2 %all-to-all-start.1 = ((bf16[64,24,2048]{2,1,0:T(8,128)(2,1)}), bf16[64,24,2048]{2,1,0:T(8,128)(2,1)}, u32[]{:S(2)}, u32[]{:S(2)}) async-start(bf16[64,24,2048]{2,1,0:T(8,128)(2,1)} %bitcast.111), calls=%async_computation.1 | async-start | bytes 12582912 | tf_op jit(solution)/shard_map/all_to_all | solution.py:156
Sparse Core Ops, SparseCore 0:
  10.8 87.2 all-gather.3
  99.9 82.5 all-gather.5
where the time goes:
time: 577 us; the launch traced here: 573 us
  blocking collectives  231 us (40%)
  waiting for transfers between devices  189 us (33%)
  local copies, waits for them, and re-layouts  69.7 us (12%)
  matrix products  27 us (5%)
  other arithmetic  24.4 us (4%)
  between operations  14.3 us (2%)
  loops' own time  11 us (2%)
  starting transfers between devices  7.43 us (1%)
    all_to_all x1, blocking collectives, body(): lax.all_to_all(outgoing, 'expert', split_axis=0, concat_axis=0, tiled=True)  186 us
    all_to_all x1, waiting for transfers between devices, body(): lax.all_to_all(result.reshape(senders, slot_total, width), 'expert', spli...  122 us
    all_gather x1, blocking collectives, body(): seg_piece = lax.all_gather(seg_local, 'expert', axis=0, tiled=True)  44.2 us
    all_gather x1, waiting for transfers between devices, body(): lax.all_gather(out_weight, 'dp', axis=0, tiled=True)  42.9 us
    all_gather x1, waiting for transfers between devices, body(): kv_piece = lax.all_gather(keys_values, 'expert', axis=0, tiled=True)  22.5 us
    another operation x3, other arithmetic  18.2 us
    unnamed x20, local copies, waits for them, and re-layouts  17.3 us
    gather x24, local copies, waits for them, and re-layouts  15.9 us
  transfers between devices with their start and end apart: 3, of which 3 were waited for; matrix products, arithmetic and copies ran while one was open for 12% of the time, Pallas kernels for 0%

commit v1 on v0

--- a/solution.py
+++ b/solution.py
@@ -1,8 +1,11 @@
+import functools
 import math
 
 import jax
 import jax.numpy as jnp
 from jax import lax
+from jax.experimental import pallas as pl
+from jax.experimental.pallas import tpu as pltpu
 from jax.sharding import PartitionSpec as P
 
 HD = 128
@@ -11,9 +14,310 @@
 TOP = 8
 PAGE = 16
 
-
 neg_big = -1e30
 norm_eps = 1e-06
+
+NZ, NY, NC = 8, 4, 2
+PLANE = NY * NC
+CAP = 24
+VMEM_LIMIT = 64 * 1024 * 1024 - 2 * 1024 * 1024
+MESH = pl.DeviceIdType.MESH
+ORDER = (0, 1, 2, -2, 3, -3, 4, -1)
+SLOT = {d: k for k, d in enumerate(ORDER)}
+
+
+def pick(table, k):
+    if isinstance(k, int):
+        return table[k]
+    value = jnp.int32(table[0])
+    for j in range(1, len(table)):
+        value = jnp.where(k == j, jnp.int32(table[j]), value)
+    return value
+
+
+def moe_kernel(
+    normed_ref, residual_ref, meta_ref, wg_hbm, wu_hbm, wd_hbm, out_ref,
+    x_buf, meta_buf, snd, arr, res, ret, part_out, part_in, acc, w_in, w_down,
+    ring_send, ring_recv, meta_send, meta_recv, disp_send, disp_recv, disp_self,
+    back_send, back_recv, back_self, part_send, part_recv, weight_sem,
+):
+    me = lax.axis_index("expert")
+    z = me // PLANE
+    pos = me % PLANE
+    rows, width = normed_ref.shape
+    fw = w_down.shape[0]
+
+    def at_z(target):
+        return {"expert": lax.rem(target + 2 * NZ, NZ) * PLANE + pos}
+
+    def at_plane(target):
+        return {"expert": z * PLANE + target}
+
+    loads = [
+        pltpu.make_async_copy(wg_hbm.at[0], w_in.at[:, pl.ds(0, fw)], weight_sem.at[0]),
+        pltpu.make_async_copy(wu_hbm.at[0], w_in.at[:, pl.ds(fw, fw)], weight_sem.at[1]),
+        pltpu.make_async_copy(wd_hbm.at[0], w_down, weight_sem.at[2]),
+    ]
+    for load in loads:
+        load.start()
+
+    barrier = pltpu.get_barrier_semaphore()
+    for d in range(1, NZ):
+        pl.semaphore_signal(barrier, inc=1, device_id=at_z(z + d), device_id_type=MESH)
+    for o in range(1, PLANE):
+        pl.semaphore_signal(
+            barrier, inc=1, device_id=at_plane(lax.rem(pos + o, PLANE)), device_id_type=MESH
+        )
+    pl.semaphore_wait(barrier, NZ - 1 + PLANE - 1)
+
+    def ring_copy(src, slot, sem, toward, first=0, count=None):
+        count = rows if count is None else count
+        return pltpu.make_async_remote_copy(
+            src_ref=src.at[pl.ds(first, count)],
+            dst_ref=x_buf.at[slot, pl.ds(first, count)],
+            send_sem=ring_send.at[sem],
+            recv_sem=ring_recv.at[sem],
+            device_id=at_z(z + toward),
+            device_id_type=MESH,
+        )
+
+    half = rows // 2
+    down = [ring_copy(normed_ref, SLOT[1], SLOT[1], -1)]
+    up = [ring_copy(normed_ref, SLOT[-1], SLOT[-1], 1)]
+    for d in (1, 2):
+        down.append(ring_copy(x_buf.at[SLOT[d]], SLOT[d + 1], SLOT[d + 1], -1))
+        up.append(ring_copy(x_buf.at[SLOT[-d]], SLOT[-d - 1], SLOT[-d - 1], 1))
+    down.append(ring_copy(x_buf.at[SLOT[3]], SLOT[4], SLOT[4], -1, 0, half))
+    up.append(ring_copy(x_buf.at[SLOT[-3]], SLOT[4], NZ, 1, half, half))
+
+    down[0].start()
+    up[0].start()
+    for k in range(1, NZ):
+        copy = pltpu.make_async_remote_copy(
+            src_ref=meta_ref,
+            dst_ref=meta_buf.at[k],
+            send_sem=meta_send,
+            recv_sem=meta_recv,
+            device_id=at_z(z - ORDER[k]),
+            device_id_type=MESH,
+        )
+        copy.start()
+    meta_buf[0] = meta_ref[...]
+
+    row_id = lax.broadcasted_iota(jnp.int32, (rows, rows), 0)
+    col_id = lax.broadcasted_iota(jnp.int32, (rows, rows), 1)
+    earlier = (row_id < col_id).astype(jnp.bfloat16)
+    first_expert = z * PLANE
+    expert_id = (first_expert + lax.broadcasted_iota(jnp.int32, (PLANE, rows), 0)).astype(
+        jnp.float32
+    )
+    slot_id = lax.broadcasted_iota(jnp.int32, (CAP, rows), 0).astype(jnp.float32)
+
+    def chosen(k, weighted):
+        meta = meta_buf[k]
+        mask = jnp.zeros((PLANE, rows), jnp.float32)
+        share = jnp.zeros((PLANE, rows), jnp.float32)
+        for n in range(TOP):
+            hit = meta[n : n + 1, :] == expert_id
+            mask = jnp.where(hit, 1.0, mask)
+            if weighted:
+                share = jnp.where(hit, meta[TOP + n : TOP + n + 1, :], share)
+        rank = jnp.dot(mask.astype(jnp.bfloat16), earlier, preferred_element_type=jnp.float32)
+        rank = jnp.where(mask > 0.5, rank, -1.0)
+        value = share if weighted else mask
+        pieces = [
+            jnp.where(rank[e : e + 1, :] == slot_id, value[e : e + 1, :], 0.0)
+            for e in range(PLANE)
+        ]
+        return jnp.concatenate(pieces, axis=0).astype(jnp.bfloat16)
+
+    def exchange(src, dst, k, send_sem, recv_sem, self_sem):
+        copies = []
+        for o in range(1, PLANE):
+            target = lax.rem(pos + o, PLANE)
+            copies.append(
+                pltpu.make_async_remote_copy(
+                    src_ref=src.at[k, target],
+                    dst_ref=dst.at[k, pos],
+                    send_sem=send_sem.at[k],
+                    recv_sem=recv_sem.at[k],
+                    device_id=at_plane(target),
+                    device_id_type=MESH,
+                )
+            )
+        own = pltpu.make_async_copy(src.at[k, pos], dst.at[k, pos], self_sem.at[k])
+        return copies, own
+
+    def start_exchange(*args):
+        copies, own = exchange(*args)
+        for copy in copies:
+            copy.start()
+        own.start()
+
+    def others(buf, k):
+        return buf.at[k, pl.ds(0, PLANE - 1)]
+
+    def wait_exchange(src, dst, k, send_sem, recv_sem, self_sem):
+        pltpu.make_async_copy(others(dst, k), others(dst, k), recv_sem.at[k]).wait()
+        pltpu.make_async_copy(src.at[k, pos], dst.at[k, pos], self_sem.at[k]).wait()
+
+    def wait_sent(src, dst, k, send_sem, recv_sem, self_sem):
+        pltpu.make_async_copy(others(src, k), others(src, k), send_sem.at[k]).wait()
+
+    disp = (disp_send, disp_recv, disp_self)
+    back = (back_send, back_recv, back_self)
+
+    def part_copy(k):
+        return pltpu.make_async_remote_copy(
+            src_ref=part_out.at[k],
+            dst_ref=part_in.at[k],
+            send_sem=part_send.at[k],
+            recv_sem=part_recv.at[k],
+            device_id=at_z(z + pick(ORDER, k)),
+            device_id_type=MESH,
+        )
+
+    def step(k, carry):
+        for r in (1, 2, 3):
+
+            @pl.when(k == r)
+            def _():
+                down[r - 1].wait_recv()
+                up[r - 1].wait_recv()
+                down[r].start()
+                up[r].start()
+                if r == 1:
+                    pltpu.make_async_copy(
+                        meta_buf.at[pl.ds(1, NZ - 1)], meta_buf.at[pl.ds(1, NZ - 1)], meta_recv
+                    ).wait()
+
+        @pl.when(k == SLOT[4])
+        def _():
+            down[3].wait_recv()
+            up[3].wait_recv()
+
+        @pl.when(k == 0)
+        def _():
+            x_buf[0] = normed_ref[...]
+
+        @pl.when(k < NZ)
+        def _():
+            sel = chosen(k, False)
+            for c in range(0, width, 512):
+                rows_out = jnp.dot(
+                    sel, x_buf[k, :, c : c + 512], preferred_element_type=jnp.float32
+                )
+                snd[k, :, :, c : c + 512] = rows_out.reshape(PLANE, CAP, 512).astype(jnp.bfloat16)
+            start_exchange(snd, arr, k, *disp)
+
+        @pl.when((k >= 1) & (k < NZ + 1))
+        def _():
+            j = k - 1
+
+            @pl.when(j == 0)
+            def _():
+                for load in loads:
+                    load.wait()
+
+            wait_exchange(snd, arr, j, *disp)
+            rows_in = arr[j].reshape(PLANE * CAP, width)
+            both = jnp.dot(rows_in, w_in[...], preferred_element_type=jnp.float32)
+            gate = both[:, :fw]
+            inner = (gate * jax.nn.sigmoid(gate) * both[:, fw:]).astype(jnp.bfloat16)
+            for c in range(0, width, 512):
+                rows_out = jnp.dot(
+                    inner, w_down[:, c : c + 512], preferred_element_type=jnp.float32
+                )
+                res[j, :, :, c : c + 512] = rows_out.reshape(PLANE, CAP, 512).astype(jnp.bfloat16)
+            start_exchange(res, ret, j, *back)
+
+        @pl.when(k >= 2)
+        def _():
+            j = k - 2
+            wait_exchange(res, ret, j, *back)
+            mix = chosen(j, True)
+            for c in range(0, width, 512):
+                part = lax.dot_general(
+                    mix,
+                    ret[j, :, :, c : c + 512].reshape(PLANE * CAP, 512),
+                    (((0,), (0,)), ((), ())),
+                    preferred_element_type=jnp.float32,
+                )
+
+                @pl.when(j == 0)
+                def _():
+                    acc[:, c : c + 512] = residual_ref[:, c : c + 512] + part
+
+                @pl.when(j > 0)
+                def _():
+                    part_out[j, :, c : c + 512] = part.astype(jnp.bfloat16)
+
+            @pl.when(j > 0)
+            def _():
+                part_copy(j).start()
+
+        return carry
+
+    lax.fori_loop(0, NZ + 2, step, 0)
+
+    def gather(k, carry):
+        part_copy(k).wait_recv()
+        acc[...] += part_in[k].astype(jnp.float32)
+        return carry
+
+    lax.fori_loop(1, NZ, gather, 0)
+    out_ref[...] = acc[...].astype(jnp.bfloat16)
+
+    for copy in down + up:
+        copy.wait_send()
+    pltpu.make_async_copy(
+        meta_buf.at[pl.ds(1, NZ - 1)], meta_buf.at[pl.ds(1, NZ - 1)], meta_send
+    ).wait()
+
+    def drain(k, carry):
+        wait_sent(snd, arr, k, *disp)
+        wait_sent(res, ret, k, *back)
+
+        @pl.when(k > 0)
+        def _():
+            part_copy(k).wait_send()
+
+        return carry
+
+    lax.fori_loop(0, NZ, drain, 0)
+
+
+def moe(normed, residual, meta, expert_gate, expert_up, expert_down):
+    rows, width = normed.shape
+    fw = expert_gate.shape[2]
+    vmem = pl.BlockSpec(memory_space=pltpu.VMEM)
+    hbm = pl.BlockSpec(memory_space=pl.ANY)
+    dma = pltpu.SemaphoreType.DMA
+    slots = pltpu.VMEM((NZ, PLANE, CAP, width), jnp.bfloat16)
+    blocks = pltpu.VMEM((NZ, rows, width), jnp.bfloat16)
+    return pl.pallas_call(
+        moe_kernel,
+        out_shape=jax.ShapeDtypeStruct((rows, width), jnp.bfloat16),
+        in_specs=[vmem, vmem, vmem, hbm, hbm, hbm],
+        out_specs=vmem,
+        scratch_shapes=[
+            blocks,
+            pltpu.VMEM((NZ, 2 * TOP, rows), jnp.float32),
+            slots, slots, slots, slots,
+            blocks, blocks,
+            pltpu.VMEM((rows, width), jnp.float32),
+            pltpu.VMEM((width, 2 * fw), jnp.bfloat16),
+            pltpu.VMEM((fw, width), jnp.bfloat16),
+            dma((NZ + 1,)), dma((NZ + 1,)), dma, dma,
+            dma((NZ,)), dma((NZ,)), dma((NZ,)),
+            dma((NZ,)), dma((NZ,)), dma((NZ,)),
+            dma((NZ,)), dma((NZ,)), dma((3,)),
+        ],
+        compiler_params=pltpu.CompilerParams(
+            collective_id=1, has_side_effects=True, vmem_limit_bytes=VMEM_LIMIT
+        ),
+        name="moe",
+    )(normed, residual, meta, expert_gate, expert_up, expert_down)
 
 
 def body(
@@ -128,44 +432,9 @@
         * lax.rsqrt(jnp.mean(residual * residual, axis=1, keepdims=True) + norm_eps)
         * norm_gain
     ).astype(jnp.bfloat16)
-    experts_total = lax.axis_size("expert")
-    capacity = min(tok_rows, (3 * tok_rows * TOP + 2 * experts_total - 1) // (2 * experts_total))
-    flat_routes = routes.reshape(-1)
-    one_hot = (flat_routes[:, None] == jnp.arange(experts_total, dtype=jnp.int32)[None, :]).astype(
-        jnp.int32
-    )
-    before = jnp.cumsum(one_hot, axis=0) - one_hot
-    slot_rank = jnp.sum(before * one_hot, axis=1)
-    target_rows = flat_routes * capacity + slot_rank
-    outgoing = (
-        jnp.zeros((experts_total * capacity, width), jnp.bfloat16)
-        .at[target_rows]
-        .set(jnp.repeat(normed, TOP, axis=0))
-    )
-    outgoing = outgoing.reshape(experts_total, capacity, width)
-    arrived_rows = lax.all_to_all(outgoing, "expert", split_axis=0, concat_axis=0, tiled=True)
-    senders = arrived_rows.shape[0]
-    slot_total = arrived_rows.shape[1]
-    flat_rows = arrived_rows.reshape(senders * slot_total, width)
-    gate_value = jnp.dot(flat_rows, expert_gate[0], preferred_element_type=jnp.float32)
-    up_value = jnp.dot(flat_rows, expert_up[0], preferred_element_type=jnp.float32)
-    hidden_units = (jax.nn.silu(gate_value) * up_value).astype(jnp.bfloat16)
-    result = jnp.dot(hidden_units, expert_down[0], preferred_element_type=jnp.float32).astype(
-        jnp.bfloat16
-    )
-    returned = lax.all_to_all(
-        result.reshape(senders, slot_total, width),
-        "expert",
-        split_axis=0,
-        concat_axis=0,
-        tiled=True,
-    )
-    picked = returned.reshape(experts_total * capacity, width)[target_rows].reshape(
-        tok_rows, TOP, width
-    )
     shares = gate_weights / jnp.sum(gate_weights, axis=1, keepdims=True)
-    combined = jnp.einsum("tk,tkd->td", shares, picked.astype(jnp.float32))
-    hidden_out = (residual + combined).astype(jnp.bfloat16)
+    meta = jnp.concatenate([routes.T.astype(jnp.float32), shares.T], axis=0)
+    hidden_out = moe(normed, residual, meta, expert_gate, expert_up, expert_down)
     return (hidden_out, cache_slots)
 
 

time: 577 us -> 450 us (0.78)
  Pallas kernels: 0 us -> 235 us
  blocking collectives: 231 us -> 44.2 us
  waiting for transfers between devices: 189 us -> 87.4 us
  local copies, waits for them, and re-layouts: 69.7 us -> 44.2 us
  matrix products: 27 us -> 7.28 us
  other arithmetic: 24.4 us -> 5.43 us
  starting transfers between devices: 7.43 us -> 0.08 us
    pallas_call x0 -> x1, Pallas kernels: none -> 235 us  [moe(): pl.pallas_call(moe_kernel, out_shape=jax.ShapeDtypeStruct((rows, width),...]
    all_to_all x1 -> x0, blocking collectives: 186 us -> none  [body(): lax.all_to_all(outgoing, 'expert', split_axis=0, concat_axis=0, tiled=True)]
    all_to_all x1 -> x0, waiting for transfers between devices: 122 us -> none  [body(): lax.all_to_all(result.reshape(senders, slot_total, width), 'expert', spli...]
    dot_general x3 -> x0, matrix products: 19.7 us -> none  [the longest x1 11.3 us: body(): jnp.dot(hidden_units, expert_down[0], preferred_element_type=jnp.float32)]
    all_gather x1, waiting for transfers between devices: 22.5 us -> 41.4 us  [body(): kv_piece = lax.all_gather(keys_values, 'expert', axis=0, tiled=True)]
    another operation x3 -> x0, other arithmetic: 18.2 us -> none
    gather x25 -> x24, local copies, waits for them, and re-layouts: 28.3 us -> 15.9 us
    scatter x1 -> x0, local copies, waits for them, and re-layouts: 10.3 us -> none  [body(): outgoing = jnp.zeros((experts_total * capacity, width), jnp.bfloat16).at[...]
  transfers between devices with their start and end apart: 3 -> 2, of which waited for: 3 -> 2; matrix products, arithmetic and copies ran while one was open for 12% -> 7% of each run, Pallas kernels for 0% -> 0%
where the time goes in v1:
time: 450 us; the launch traced here: 448 us
  Pallas kernels  235 us (52%)
  waiting for transfers between devices  87.4 us (19%)
  local copies, waits for them, and re-layouts  44.2 us (10%)
  blocking collectives  44.2 us (10%)
  between operations  14.3 us (3%)
  loops' own time  10.8 us (2%)
  matrix products  7.28 us (2%)
  other arithmetic  5.43 us (1%)
    pallas_call x1, Pallas kernels, moe(): pl.pallas_call(moe_kernel, out_shape=jax.ShapeDtypeStruct((rows, width),...  235 us
    all_gather x1, waiting for transfers between devices, body(): lax.all_gather(out_weight, 'dp', axis=0, tiled=True)  44.6 us
    all_gather x1, blocking collectives, body(): seg_piece = lax.all_gather(seg_local, 'expert', axis=0, tiled=True)  44.2 us
    all_gather x1, waiting for transfers between devices, body(): kv_piece = lax.all_gather(keys_values, 'expert', axis=0, tiled=True)  41.4 us
    unnamed x18, local copies, waits for them, and re-layouts  15.9 us
    gather x24, local copies, waits for them, and re-layouts  15.9 us
    another operation x1, loops' own time, body(): lax.scan(advance, softmax_state, (kv_steps, seg_steps, block_starts))  10.5 us
    dynamic_slice x17, local copies, waits for them, and re-layouts, body(): lax.scan(advance, softmax_state, (kv_steps, seg_steps, block_starts))  10.3 us
  transfers between devices with their start and end apart: 2, of which 2 were waited for; matrix products, arithmetic and copies ran while one was open for 7% of the time, Pallas kernels for 0%

profile of v1, /device:TPU:1, one launch (start us, length us, event | category | flops | bytes accessed | tf_op | source)
XLA Modules:
  0.0 448.3 jit_solution(13635340976178378547)
XLA Ops:
  8.7 1.3 copy.31
  10.3 44.2 %all-gather = s32[1,8192]{1,0:T(1,128)S(1)} all-gather(s32[1,128]{1,0:T(1,128)S(1)} %copy-done.2), channel_id=2, replica_groups=mesh['dp'=4,'expert'=64] {'expert'}, dimensions={1}, use_global_device_ids=true | all-gather | bytes 33280 | tf_op jit(solution)/shard_map/all_gather | solution.py:402
  56.7 41.4 %all-gather.4.cloned.1.call-done = bf16[8192,512]{1,0:T(8,128)(2,1)} async-done(((bf16[128,512]{1,0:T(8,128)(2,1)}), bf16[8192,512]{1,0:T(8,128)(2,1)}) %all-gather.4.cloned.1.call-update) | async-done | bytes 8388624 | tf_op jit(solution)/shard_map/all_gather | solution.py:401
  98.1 12.4 %copy.32 = bf16[16,512,512]{1,2,0:T(8,128)(2,1)} copy(bf16[16,512,512]{2,1,0:T(8,128)(2,1)} %bitcast.62) | data formatting | bytes 16777216
  110.6 26.7 %while.19 = (s32[]{:T(128)}, f32[128,2,8]{0,2,1:T(8,128)S(1)}, f32[128,2,8]{0,2,1:T(8,128)S(1)}, f32[128,2,8,128]{3,0,2,1:T(8,128)S(1)}, s32[16]{0:T(128)S(1)}, ...) while((s32[]{:T(128)}, f32[128,2,8]{0,2,1:T(8,128)S(1)}, ...), condition=%wide.region_5.6_spmd.clone.clone, body=%wide.region_0.5_spmd.clone.sunk.clone | while | flops 551228032 | bytes 18232104 | solution.py:409
  111.9 5.7 %conditional.4 = ((f32[128,2,8]{0,2,1:T(8,128)S(1)}, f32[128,2,8]{0,2,1:T(8,128)S(1)}, f32[128,2,8,128]{3,0,2,1:T(8,128)S(1)})) conditional(s32[]{:T(128)} %convert_element_type.46, (f32[128,2,8]{0,2,1:T(8,128)S(1)}, f32[128,2,8]{0,2,1:T(8,128)S(1)}, f32[128,2,8,128]{3,0,2,1:T(8,128)S(1)}) %tuple.65, (s32[]{:T(128)}, s32[]{:T(128)}, ...), branch_computations={%region_1.1_spmd, %region_2.4_spmd} | conditional | flops 551228032 | bytes 18231344 | solution.py:391
  112.8 1.1 dynamic-slice_bitcast_fusion
  114.0 0.8 fusion.2
  114.9 1.0 fusion.4
  115.9 1.7 fusion.11
  137.8 44.6 %all-gather.6.cloned.1.call-done = bf16[2048,2048]{1,0:T(8,128)(2,1)} async-done(((bf16[512,2048]{1,0:T(8,128)(2,1)}), bf16[2048,2048]{1,0:T(8,128)(2,1)}) %all-gather.6.cloned.1.call-update) | async-done | bytes 8388624 | tf_op jit(solution)/shard_map/all_gather | solution.py:426
  182.4 4.8 %multiply_reduce_fusion = (f32[128]{0:T(128)S(1)}, f32[128,2048]{1,0:T(8,128)S(1)}) fusion(bf16[128,2048]{0,1:T(8,128)(2,1)S(1)} %bitcast.64, bf16[2048,2048]{1,0:T(8,128)(2,1)} %all-gather.6.cloned.1.call-done, bf16[128,2048]{1,0:T(8,128)(2,1)S(1)} %copy-done.1), kind=kOutput, calls=%fused_computation.24 | convolution fusion | flops 1074790272 | bytes 10486272 | tf_op jit(solution)/shard_map/dot_general | solution.py:424
  187.2 1.2 multiply_convert_fusion.normed_ref
  188.3 234.6 %moe.1 = bf16[128,2048]{1,0:T(8,128)(2,1)} custom-call(bf16[128,2048]{1,0:T(8,128)(2,1)} %multiply_convert_fusion.normed_ref, f32[128,2048]{1,0:T(8,128)} %copy-done, f32[16,128]{1,0:T(8,128)} %pad_maximum_fusion.meta_ref, bf16[1,2048,384]{2,1,0:T(8,128)(2,1)} %wg_hbm.1, bf16[1,2048,384]{2,1,0:T(8,128)(2,1)} %wu_hbm.1, bf16[1,384,2048]{2,1,0:T(8,128)(2,1)} %wd_hbm.1), custom_call_target="tpu_custom_call" | custom-call | tf_op jit(solution)/shard_map/moe/pallas_call | solution.py:298
  422.9 15.9 %while.18 = (s32[]{:T(128)}, bf16[8192,512]{1,0:T(8,128)(2,1)}, s32[8,2]{0,1:T(2,128)S(1)}, bf16[8,16,512]{2,1,0:T(8,128)(2,1)S(1)}) while((s32[]{:T(128)}, bf16[8192,512]{1,0:T(8,128)(2,1)}, s32[8,2]{0,1:T(2,128)S(1)}, bf16[8,16,512]{2,1,0:T(8,128)(2,1)S(1)}) %tuple.73), condition=%wide.while_cond.clone, body=%wide.while_body.sunk.clone | while | flops 2 | bytes 32857 | solution.py:415
  423.5 1.4 bitcast_dynamic-update-slice_fusion.3
  425.5 1.4 bitcast_dynamic-update-slice_fusion.3
  427.5 1.4 bitcast_dynamic-update-slice_fusion.3
  429.5 1.4 bitcast_dynamic-update-slice_fusion.3
  431.4 1.4 bitcast_dynamic-update-slice_fusion.3
  433.4 1.4 bitcast_dynamic-update-slice_fusion.3
  435.4 1.4 bitcast_dynamic-update-slice_fusion.3
  437.4 1.4 bitcast_dynamic-update-slice_fusion.3
  439.5 1.9 copy.69
  (111 shorter events, 21.3 us)
Async XLA Ops:
  7.2 3.1 copy-start.2
  7.2 48.7 %copy-start.6 = (s32[1,512]{1,0:T(1,128)S(1)}, s32[1,512]{1,0:T(1,128)}, u32[]{:S(2)}) copy-start(s32[1,512]{1,0:T(1,128)} %param.22) | copy-start | bytes 6148
  7.2 48.9 %copy-start.3 = (f32[128,8]{0,1:T(8,128)S(1)}, f32[128,8]{0,1:T(8,128)}, u32[]{:S(2)}) copy-start(f32[128,8]{0,1:T(8,128)} %param.21) | copy-start | bytes 12292
  7.2 48.9 %copy-start.5 = (s32[128,8]{0,1:T(8,128)S(1)}, s32[128,8]{0,1:T(8,128)}, u32[]{:S(2)}) copy-start(s32[128,8]{0,1:T(8,128)} %param.20) | copy-start | bytes 12292
  7.2 90.9 %all-gather.4.cloned.1.call-start = ((), (), s32[]{:S(2)}) async-start(), calls=%async_computation | async-start | bytes 8519680 | tf_op jit(solution)/shard_map/all_gather | solution.py:401
  7.9 174.4 %all-gather.6.cloned.1.call-start = ((), (), s32[]{:S(2)}) async-start(), calls=%async_computation.1 | async-start | bytes 10485760 | tf_op jit(solution)/shard_map/all_gather | solution.py:426
  110.6 71.7 %copy-start.1 = (bf16[128,2048]{1,0:T(8,128)(2,1)S(1)}, bf16[128,2048]{1,0:T(8,128)(2,1)}, u32[]{:S(2)}) copy-start(bf16[128,2048]{1,0:T(8,128)(2,1)} %param.16) | copy-start | bytes 1572868
  182.4 4.8 %copy-start.4 = (f32[2048]{0:T(1024)S(1)}, f32[2048]{0:T(1024)}, u32[]{:S(2)}) copy-start(f32[2048]{0:T(1024)} %param.24) | copy-start | bytes 24580
  187.1 1.2 copy-start
Sparse Core Ops, SparseCore 0:
  10.8 87.2 all-gather.3
  99.9 82.3 all-gather.5

commit v2 on v1

--- a/solution.py
+++ b/solution.py
@@ -320,6 +320,156 @@
     )(normed, residual, meta, expert_gate, expert_up, expert_down)
 
 
+def spread_kernel(
+    seg_ref, weight_ref, seg_out, weight_out,
+    seg_buf, seg_send, seg_recv, own_sem, x_send, x_recv, core_send, core_recv,
+):
+    members = seg_out.shape[0]
+    me = lax.axis_index("expert")
+    col = lax.axis_index("dp")
+    n_dp = lax.axis_size("dp")
+    block = weight_ref.shape[0]
+    half = block // NC
+    core = lax.rem(me, NC)
+
+    def peer(o):
+        return {"expert": lax.rem(me + o, members)}
+
+    def at_dp(o):
+        return {"dp": lax.rem(col + o, n_dp)}
+
+    barrier = pltpu.get_barrier_semaphore()
+    for o in range(1, n_dp):
+        pl.semaphore_signal(barrier, inc=1, device_id=at_dp(o), device_id_type=MESH)
+
+    def greet(o, carry):
+        pl.semaphore_signal(barrier, inc=1, device_id=peer(o), device_id_type=MESH)
+        return carry
+
+    lax.fori_loop(1, members, greet, 0)
+    pl.semaphore_wait(barrier, members - 1 + n_dp - 1)
+
+    mine = pl.ds(pl.multiple_of(core * half, half), half)
+    hops = (1, 3, 2)
+
+    def rows_of(source):
+        return pl.ds(pl.multiple_of(source * block + core * half, half), half)
+
+    across = {}
+    for o in hops:
+        across[o] = pltpu.make_async_remote_copy(
+            src_ref=weight_ref.at[mine],
+            dst_ref=weight_out.at[rows_of(col)],
+            send_sem=x_send.at[o],
+            recv_sem=x_recv.at[o],
+            device_id=at_dp(o),
+            device_id_type=MESH,
+        )
+        across[o].start()
+
+    def send_seg(o, carry):
+        pltpu.make_async_remote_copy(
+            src_ref=seg_ref,
+            dst_ref=seg_buf.at[me],
+            send_sem=seg_send,
+            recv_sem=seg_recv,
+            device_id=peer(o),
+            device_id_type=MESH,
+        ).start()
+        return carry
+
+    lax.fori_loop(1, members, send_seg, 0)
+    own = pltpu.make_async_copy(
+        weight_ref, weight_out.at[pl.ds(pl.multiple_of(col * block, block), block)], own_sem
+    )
+    own.start()
+    seg_buf[me] = seg_ref[...]
+
+    over = {}
+    for o in hops:
+        across[o].wait_recv()
+        came = rows_of(lax.rem(col - o + n_dp, n_dp))
+        over[o] = pltpu.make_async_remote_copy(
+            src_ref=weight_out.at[came],
+            dst_ref=weight_out.at[came],
+            send_sem=core_send.at[o],
+            recv_sem=core_recv.at[o],
+            device_id={"expert": me + 1 - 2 * core},
+            device_id_type=MESH,
+        )
+        over[o].start()
+
+    others = seg_buf.at[pl.ds(0, members - 1)]
+    pltpu.make_async_copy(others, others, seg_recv).wait()
+    seg_out[...] = seg_buf[...]
+    pltpu.make_async_copy(others, others, seg_send).wait()
+    own.wait()
+    for o in hops:
+        across[o].wait_send()
+        over[o].wait_send()
+        over[o].wait_recv()
+
+
+def spread(seg_rows, out_weight):
+    members = lax.axis_size("expert")
+    n_dp = lax.axis_size("dp")
+    block, width = out_weight.shape
+    vmem = pl.BlockSpec(memory_space=pltpu.VMEM)
+    hbm = pl.BlockSpec(memory_space=pl.ANY)
+    dma = pltpu.SemaphoreType.DMA
+    seg_shape = (members,) + seg_rows.shape
+    return pl.pallas_call(
+        spread_kernel,
+        out_shape=(
+            jax.ShapeDtypeStruct(seg_shape, jnp.int32),
+            jax.ShapeDtypeStruct((n_dp * block, width), out_weight.dtype),
+        ),
+        in_specs=[vmem, vmem],
+        out_specs=(vmem, hbm),
+        scratch_shapes=[
+            pltpu.VMEM(seg_shape, jnp.int32),
+            dma, dma, dma,
+            dma((n_dp,)), dma((n_dp,)), dma((n_dp,)), dma((n_dp,)),
+        ],
+        compiler_params=pltpu.CompilerParams(collective_id=2, has_side_effects=True),
+        cost_estimate=pl.CostEstimate(flops=0, bytes_accessed=150_000_000, transcendentals=0),
+        name="spread",
+    )(seg_rows, out_weight)
+
+
+def pages_kernel(page_ref, rows_hbm, out_ref, sems):
+    count = out_ref.shape[0]
+    last = rows_hbm.shape[0] // PAGE - 1
+    copies = []
+    for n in range(count):
+        page = jnp.minimum(jnp.maximum(page_ref[n], 0), last)
+        copies.append(
+            pltpu.make_async_copy(
+                rows_hbm.at[pl.ds(pl.multiple_of(page * PAGE, PAGE), PAGE)],
+                out_ref.at[n],
+                sems.at[n],
+            )
+        )
+        copies[-1].start()
+    for copy in copies:
+        copy.wait()
+
+
+def take_pages(pages, rows):
+    count = pages.shape[0]
+    return pl.pallas_call(
+        pages_kernel,
+        out_shape=jax.ShapeDtypeStruct((count, PAGE, rows.shape[1]), rows.dtype),
+        in_specs=[
+            pl.BlockSpec(memory_space=pltpu.SMEM),
+            pl.BlockSpec(memory_space=pl.ANY),
+        ],
+        out_specs=pl.BlockSpec(memory_space=pltpu.VMEM),
+        scratch_shapes=[pltpu.SemaphoreType.DMA((count,))],
+        name="pages",
+    )(pages, rows)
+
+
 def body(
     hidden_in,
     queries,
@@ -395,11 +545,10 @@
         jnp.zeros((tok_rows, HK, groups), jnp.float32),
         jnp.zeros((tok_rows, HK, groups, HD), jnp.float32),
     )
-    start_cache = jnp.zeros((slot_count, PAGE, keys_values.shape[1]), jnp.bfloat16)
     softmax_state = start_state
-    cache_slots = start_cache
     kv_piece = lax.all_gather(keys_values, "expert", axis=0, tiled=True)
-    seg_piece = lax.all_gather(seg_local, "expert", axis=0, tiled=True)
+    seg_all, weight_all = spread(jnp.broadcast_to(seg_local[None, :], (8, tok_rows)), out_weight)
+    seg_piece = seg_all[:, 0, :].reshape(-1)
     piece_rows = kv_piece.shape[0]
     block_rows = math.gcd(piece_rows, 512)
     block_count = piece_rows // block_rows
@@ -407,23 +556,14 @@
     seg_steps = seg_piece.reshape(block_count, block_rows)
     block_starts = block_rows * jnp.arange(block_count, dtype=jnp.int32)
     softmax_state, _ = lax.scan(advance, softmax_state, (kv_steps, seg_steps, block_starts))
-    local_row = page_of_slot * PAGE
-    inside = (local_row >= 0) & (local_row < piece_rows)
-    safe_row = jnp.clip(local_row, 0, piece_rows - PAGE)
-
-    def take_page(row_start):
-        return lax.dynamic_slice_in_dim(kv_piece, row_start, PAGE, 0)
-
-    page_rows = jax.vmap(take_page)(safe_row)
-    cache_slots = jnp.where(inside[:, None, None], page_rows, cache_slots)
-    final_state, cache_slots = (softmax_state, cache_slots)
-    running_max, running_sum, running_acc = final_state
+    cache_slots = take_pages(page_of_slot, kv_piece)
+    running_max, running_sum, running_acc = softmax_state
     attended = (
         (running_acc / running_sum[..., None]).reshape(tok_rows, HQ * HD).astype(jnp.bfloat16)
     )
     projected = jnp.dot(
         attended,
-        lax.all_gather(out_weight, "dp", axis=0, tiled=True),
+        weight_all,
         preferred_element_type=jnp.float32,
     )
     residual = hidden_in.astype(jnp.float32) + projected

time: 450 us -> 435 us (0.967)
  Pallas kernels: 235 us -> 348 us
  waiting for transfers between devices: 87.4 us -> 19.7 us
  blocking collectives: 44.2 us -> 0 us
  local copies, waits for them, and re-layouts: 44.2 us -> 28.4 us
    pallas_call x0 -> x2, Pallas kernels: none -> 68.2 us  [the longest x1 65.8 us: spread(): pl.pallas_call(spread_kernel, out_shape=(jax.ShapeDtypeStruct(seg_shape,...]
    pallas_call x1, Pallas kernels: 235 us -> 279 us  [moe(): pl.pallas_call(moe_kernel, out_shape=jax.ShapeDtypeStruct((rows, width),...]
    all_gather x1 -> x0, waiting for transfers between devices: 44.6 us -> none  [body(): lax.all_gather(out_weight, 'dp', axis=0, tiled=True)]
    all_gather x1 -> x0, blocking collectives: 44.2 us -> none  [body(): seg_piece = lax.all_gather(seg_local, 'expert', axis=0, tiled=True)]
    all_gather x1, waiting for transfers between devices: 41.4 us -> 19 us  [body(): kv_piece = lax.all_gather(keys_values, 'expert', axis=0, tiled=True)]
    gather x24 -> x0, local copies, waits for them, and re-layouts: 15.9 us -> none
  transfers between devices with their start and end apart: 2 -> 1, of which waited for: 2 -> 1; matrix products, arithmetic and copies ran while one was open for 7% -> 1% of each run, Pallas kernels for 0% -> 15%
where the time goes in v2:
time: 435 us; the launch traced here: 433 us
  Pallas kernels  348 us (80%)
  local copies, waits for them, and re-layouts  28.4 us (7%)
  waiting for transfers between devices  19.7 us (5%)
  between operations  14.2 us (3%)
  loops' own time  11.2 us (3%)
  matrix products  7.31 us (2%)
  other arithmetic  4.51 us (1%)
    pallas_call x1, Pallas kernels, moe(): pl.pallas_call(moe_kernel, out_shape=jax.ShapeDtypeStruct((rows, width),...  279 us
    pallas_call x1, Pallas kernels, spread(): pl.pallas_call(spread_kernel, out_shape=(jax.ShapeDtypeStruct(seg_shape,...  65.8 us
    all_gather x1, waiting for transfers between devices, body(): kv_piece = lax.all_gather(keys_values, 'expert', axis=0, tiled=True)  19 us
    unnamed x18, local copies, waits for them, and re-layouts  14.8 us
    another operation x1, loops' own time, body(): lax.scan(advance, softmax_state, (kv_steps, seg_steps, block_starts))  10.8 us
    dynamic_slice x17, local copies, waits for them, and re-layouts, body(): lax.scan(advance, softmax_state, (kv_steps, seg_steps, block_starts))  9.79 us
  transfers between devices with their start and end apart: 1, of which 1 were waited for; matrix products, arithmetic and copies ran while one was open for 1% of the time, Pallas kernels for 15%

profile of v2, /device:TPU:1, one launch (start us, length us, event | category | flops | bytes accessed | tf_op | source)
XLA Modules:
  0.0 433.1 jit_solution(15924954671374040225)
XLA Ops:
  7.2 0.7 all-gather.2.cloned.1.call-update
  7.9 1.3 copy.25
  9.5 1.3 broadcast_in_dim.57.seg_ref
  10.8 65.8 %spread.1 = (s32[64,8,128]{2,1,0:T(8,128)}, bf16[2048,2048]{1,0:T(8,128)(2,1)}) custom-call(s32[8,128]{1,0:T(8,128)} %broadcast_in_dim.57.seg_ref, bf16[512,2048]{1,0:T(8,128)(2,1)} %weight_ref.1), custom_call_target="tpu_custom_call" | custom-call | bytes 150000000 | tf_op jit(solution)/shard_map/spread/pallas_call | solution.py:421
  76.6 1.0 slice_reduce_fusion
  78.4 0.7 select_reduce_fusion.page_ref
  79.1 19.0 %all-gather.2.cloned.1.call-done.rows_hbm = bf16[8192,512]{1,0:T(8,128)(2,1)} async-done(((bf16[128,512]{1,0:T(8,128)(2,1)}), bf16[8192,512]{1,0:T(8,128)(2,1)}) %all-gather.2.cloned.1.call-update) | async-done | bytes 8388624 | tf_op jit(solution)/shard_map/all_gather | solution.py:549
  98.1 12.3 %copy.26 = bf16[16,512,512]{1,2,0:T(8,128)(2,1)} copy(bf16[16,512,512]{2,1,0:T(8,128)(2,1)} %bitcast.50) | data formatting | bytes 16777216
  110.6 26.5 %while.15 = (s32[]{:T(128)}, f32[128,2,8]{0,2,1:T(8,128)S(1)}, f32[128,2,8]{0,2,1:T(8,128)S(1)}, f32[128,2,8,128]{3,0,2,1:T(8,128)S(1)}, s32[16]{0:T(128)S(1)}, ...) while((s32[]{:T(128)}, f32[128,2,8]{0,2,1:T(8,128)S(1)}, ...), condition=%wide.region_5.6_spmd.clone, body=%wide.region_0.5_spmd.clone.sunk | while | flops 551228032 | bytes 18232120 | solution.py:558
  111.8 5.6 %conditional.3 = ((f32[128,2,8]{0,2,1:T(8,128)S(1)}, f32[128,2,8]{0,2,1:T(8,128)S(1)}, f32[128,2,8,128]{3,0,2,1:T(8,128)S(1)})) conditional(s32[]{:T(128)} %convert_element_type.45, (f32[128,2,8]{0,2,1:T(8,128)S(1)}, f32[128,2,8]{0,2,1:T(8,128)S(1)}, f32[128,2,8,128]{3,0,2,1:T(8,128)S(1)}) %tuple.46, (s32[]{:T(128)}, s32[]{:T(128)}, ...), branch_computations={%region_1.1_spmd, %region_2.4_spmd} | conditional | flops 551228032 | bytes 18231344 | solution.py:541
  111.9 1.1 dynamic-slice_bitcast_fusion
  113.0 0.6 iota_add_fusion
  113.9 0.8 fusion.2
  114.7 1.0 fusion.4
  115.8 1.7 fusion.11
  121.4 0.6 dynamic_slice.26
  122.7 0.6 dynamic_slice.26
  124.0 0.6 dynamic_slice.26
  125.3 0.6 dynamic_slice.26
  137.5 4.8 %multiply_reduce_fusion = (f32[128]{0:T(128)S(1)}, f32[128,2048]{1,0:T(8,128)S(1)}) fusion(bf16[128,2048]{0,1:T(8,128)(2,1)S(1)} %bitcast.53, bf16[2048,2048]{1,0:T(8,128)(2,1)} %get-tuple-element.155, bf16[128,2048]{1,0:T(8,128)(2,1)} %param.16), kind=kOutput, calls=%fused_computation.22 | convolution fusion | flops 1074790272 | bytes 10486272 | tf_op jit(solution)/shard_map/dot_general | solution.py:564
  142.4 1.2 multiply_convert_fusion.normed_ref
  143.5 279.5 %moe.1 = bf16[128,2048]{1,0:T(8,128)(2,1)} custom-call(bf16[128,2048]{1,0:T(8,128)(2,1)} %multiply_convert_fusion.normed_ref, f32[128,2048]{1,0:T(8,128)} %copy-done, f32[16,128]{1,0:T(8,128)} %pad_maximum_fusion.meta_ref, bf16[1,2048,384]{2,1,0:T(8,128)(2,1)} %wg_hbm.1, bf16[1,2048,384]{2,1,0:T(8,128)(2,1)} %wu_hbm.1, bf16[1,384,2048]{2,1,0:T(8,128)(2,1)} %wd_hbm.1), custom_call_target="tpu_custom_call" | custom-call | tf_op jit(solution)/shard_map/moe/pallas_call | solution.py:298
  423.0 2.4 pages.1
  425.4 0.8 copy.57
  (79 shorter events, 9.5 us)
Async XLA Ops:
  7.2 70.5 %copy-start.3 = (f32[128,8]{0,1:T(8,128)S(1)}, f32[128,8]{0,1:T(8,128)}, u32[]{:S(2)}) copy-start(f32[128,8]{0,1:T(8,128)} %param.21) | copy-start | bytes 12292
  7.2 70.6 %copy-start.5 = (s32[128,8]{0,1:T(8,128)S(1)}, s32[128,8]{0,1:T(8,128)}, u32[]{:S(2)}) copy-start(s32[128,8]{0,1:T(8,128)} %param.20) | copy-start | bytes 12292
  7.2 71.2 %copy-start.6 = (s32[1,512]{1,0:T(1,128)S(1)}, s32[1,512]{1,0:T(1,128)}, u32[]{:S(2)}) copy-start(s32[1,512]{1,0:T(1,128)} %param.22) | copy-start | bytes 6148
  7.2 90.9 %all-gather.2.cloned.1.call-start = ((), (), s32[]{:S(2)}) async-start(), calls=%async_computation | async-start | bytes 8519680 | tf_op jit(solution)/shard_map/all_gather | solution.py:549
  98.1 12.4 %copy-start.2 = (s32[1,128]{1,0:T(1,128)S(1)}, s32[1,128]{1,0:T(1,128)}, u32[]{:S(2)}) copy-start(s32[1,128]{1,0:T(1,128)} %param.19) | copy-start | bytes 1540
  137.5 4.8 %copy-start.4 = (f32[2048]{0:T(1024)S(1)}, f32[2048]{0:T(1024)}, u32[]{:S(2)}) copy-start(f32[2048]{0:T(1024)} %param.24) | copy-start | bytes 24580
  142.3 1.2 copy-start
  423.0 2.4 copy-start.1
Sparse Core Ops, SparseCore 0:
  10.8 87.2 all-gather.1

commit v3 on v2

--- a/solution.py
+++ b/solution.py
@@ -20,6 +20,7 @@
 NZ, NY, NC = 8, 4, 2
 PLANE = NY * NC
 CAP = 24
+LAG = 2
 VMEM_LIMIT = 64 * 1024 * 1024 - 2 * 1024 * 1024
 MESH = pl.DeviceIdType.MESH
 ORDER = (0, 1, 2, -2, 3, -3, 4, -1)
@@ -210,9 +211,9 @@
                 snd[k, :, :, c : c + 512] = rows_out.reshape(PLANE, CAP, 512).astype(jnp.bfloat16)
             start_exchange(snd, arr, k, *disp)
 
-        @pl.when((k >= 1) & (k < NZ + 1))
+        @pl.when((k >= LAG) & (k < NZ + LAG))
         def _():
-            j = k - 1
+            j = k - LAG
 
             @pl.when(j == 0)
             def _():
@@ -231,9 +232,9 @@
                 res[j, :, :, c : c + 512] = rows_out.reshape(PLANE, CAP, 512).astype(jnp.bfloat16)
             start_exchange(res, ret, j, *back)
 
-        @pl.when(k >= 2)
+        @pl.when(k >= 2 * LAG)
         def _():
-            j = k - 2
+            j = k - 2 * LAG
             wait_exchange(res, ret, j, *back)
             mix = chosen(j, True)
             for c in range(0, width, 512):
@@ -258,7 +259,7 @@
 
         return carry
 
-    lax.fori_loop(0, NZ + 2, step, 0)
+    lax.fori_loop(0, NZ + 2 * LAG, step, 0)
 
     def gather(k, carry):
         part_copy(k).wait_recv()
@@ -537,7 +538,7 @@
     def advance(carried, inputs):
         kv_block, seg_block, block_start = inputs
         row_count = kv_block.shape[0]
-        needed = block_start <= last_pos
+        needed = (block_start <= last_pos) & (seg_block[-1] >= seg_local[0])
         return (lax.cond(needed, attend_block, keep_state, carried, inputs), None)
 
     start_state = (

time: 435 us -> 427 us (0.982)
  Pallas kernels: 348 us -> 319 us
  local copies, waits for them, and re-layouts: 28.4 us -> 39.4 us
  loops' own time: 11.2 us -> 21 us
    pallas_call x1, Pallas kernels: 279 us -> 251 us  [moe(): pl.pallas_call(moe_kernel, out_shape=jax.ShapeDtypeStruct((rows, width),...]
    slice x0 -> x16, local copies, waits for them, and re-layouts: none -> 10.3 us  [advance(): needed = (block_start <= last_pos) & (seg_block[-1] >= seg_local[0])]
    another operation x1, loops' own time: 10.8 us -> 20.7 us  [body(): lax.scan(advance, softmax_state, (kv_steps, seg_steps, block_starts))]
    dynamic_slice x17 -> x32, local copies, waits for them, and re-layouts: 9.79 us -> 10.4 us  [body(): lax.scan(advance, softmax_state, (kv_steps, seg_steps, block_starts))]
    unnamed x18 -> x20, local copies, waits for them, and re-layouts: 14.8 us -> 14.8 us
where the time goes in v3:
time: 427 us; the launch traced here: 425 us
  Pallas kernels  319 us (75%)
  local copies, waits for them, and re-layouts  39.4 us (9%)
  loops' own time  21 us (5%)
  waiting for transfers between devices  19.7 us (5%)
  between operations  14.3 us (3%)
  matrix products  7.31 us (2%)
  other arithmetic  4.47 us (1%)
    pallas_call x1, Pallas kernels, moe(): pl.pallas_call(moe_kernel, out_shape=jax.ShapeDtypeStruct((rows, width),...  251 us
    pallas_call x1, Pallas kernels, spread(): pl.pallas_call(spread_kernel, out_shape=(jax.ShapeDtypeStruct(seg_shape,...  65.8 us
    another operation x1, loops' own time, body(): lax.scan(advance, softmax_state, (kv_steps, seg_steps, block_starts))  20.7 us
    all_gather x1, waiting for transfers between devices, body(): kv_piece = lax.all_gather(keys_values, 'expert', axis=0, tiled=True)  19 us
    unnamed x20, local copies, waits for them, and re-layouts  14.8 us
    dynamic_slice x32, local copies, waits for them, and re-layouts, body(): lax.scan(advance, softmax_state, (kv_steps, seg_steps, block_starts))  10.4 us
    slice x16, local copies, waits for them, and re-layouts, advance(): needed = (block_start <= last_pos) & (seg_block[-1] >= seg_local[0])  10.3 us
  transfers between devices with their start and end apart: 1, of which 1 were waited for; matrix products, arithmetic and copies ran while one was open for 1% of the time, Pallas kernels for 15%

profile of v3, /device:TPU:1, one launch (start us, length us, event | category | flops | bytes accessed | tf_op | source)
XLA Modules:
  0.0 425.3 jit_solution(1450607544802749969)
XLA Ops:
  7.2 0.7 all-gather.2.cloned.1.call-update
  7.9 1.3 copy.25
  9.5 1.3 broadcast_in_dim.53.seg_ref
  10.8 65.8 %spread.1 = (s32[64,8,128]{2,1,0:T(8,128)}, bf16[2048,2048]{1,0:T(8,128)(2,1)}) custom-call(s32[8,128]{1,0:T(8,128)} %broadcast_in_dim.53.seg_ref, bf16[512,2048]{1,0:T(8,128)(2,1)} %weight_ref.1), custom_call_target="tpu_custom_call" | custom-call | bytes 150000000 | tf_op jit(solution)/shard_map/spread/pallas_call | solution.py:422
  76.6 1.0 slice_reduce_fusion
  78.4 0.7 select_reduce_fusion.page_ref
  79.1 19.0 %all-gather.2.cloned.1.call-done.rows_hbm = bf16[8192,512]{1,0:T(8,128)(2,1)} async-done(((bf16[128,512]{1,0:T(8,128)(2,1)}), bf16[8192,512]{1,0:T(8,128)(2,1)}) %all-gather.2.cloned.1.call-update) | async-done | bytes 8388624 | tf_op jit(solution)/shard_map/all_gather | solution.py:550
  98.1 12.3 %copy.26 = bf16[16,512,512]{1,2,0:T(8,128)(2,1)} copy(bf16[16,512,512]{2,1,0:T(8,128)(2,1)} %bitcast.59) | data formatting | bytes 16777216
  110.6 47.3 %while.15 = (s32[]{:T(128)}, f32[128,2,8]{0,2,1:T(8,128)S(1)}, f32[128,2,8]{0,2,1:T(8,128)S(1)}, f32[128,2,8,128]{3,0,2,1:T(8,128)S(1)}, s32[16]{0:T(128)S(1)}, ...) while((s32[]{:T(128)}, f32[128,2,8]{0,2,1:T(8,128)S(1)}, ...), condition=%wide.region_5.6_spmd.clone, body=%wide.region_0.5_spmd.clone.sunk | while | flops 551228032 | bytes 18232180 | solution.py:559
  113.1 5.6 %conditional.3 = ((f32[128,2,8]{0,2,1:T(8,128)S(1)}, f32[128,2,8]{0,2,1:T(8,128)S(1)}, f32[128,2,8,128]{3,0,2,1:T(8,128)S(1)})) conditional(s32[]{:T(128)} %convert_element_type.44, (f32[128,2,8]{0,2,1:T(8,128)S(1)}, f32[128,2,8]{0,2,1:T(8,128)S(1)}, f32[128,2,8,128]{3,0,2,1:T(8,128)S(1)}) %tuple.44, (s32[]{:T(128)}, s32[]{:T(128)}, ...), branch_computations={%region_1.1_spmd, %region_2.4_spmd} | conditional | flops 551228032 | bytes 18227244 | solution.py:542
  114.0 1.1 dynamic-slice_bitcast_fusion
  115.1 0.8 fusion.2
  116.0 1.0 fusion.4
  117.0 1.7 fusion.11
  118.8 0.6 dynamic-slice.2
  126.6 0.6 dynamic-slice.2
  129.2 0.6 dynamic-slice.2
  137.1 0.6 dynamic-slice.2
  139.7 0.6 dynamic-slice.2
  158.4 4.7 %multiply_reduce_fusion = (f32[128]{0:T(128)S(1)}, f32[128,2048]{1,0:T(8,128)S(1)}) fusion(bf16[128,2048]{0,1:T(8,128)(2,1)S(1)} %bitcast.62, bf16[2048,2048]{1,0:T(8,128)(2,1)} %get-tuple-element.133, bf16[128,2048]{1,0:T(8,128)(2,1)S(1)} %copy-done.2), kind=kOutput, calls=%fused_computation.22 | convolution fusion | flops 1074790272 | bytes 10486272 | tf_op jit(solution)/shard_map/dot_general | solution.py:565
  163.2 1.2 multiply_convert_fusion.normed_ref
  164.4 250.9 %moe.1 = bf16[128,2048]{1,0:T(8,128)(2,1)} custom-call(bf16[128,2048]{1,0:T(8,128)(2,1)} %multiply_convert_fusion.normed_ref, f32[128,2048]{1,0:T(8,128)} %copy-done, f32[16,128]{1,0:T(8,128)} %pad_maximum_fusion.meta_ref, bf16[1,2048,384]{2,1,0:T(8,128)(2,1)} %wg_hbm.1, bf16[1,2048,384]{2,1,0:T(8,128)(2,1)} %wu_hbm.1, bf16[1,384,2048]{2,1,0:T(8,128)(2,1)} %wd_hbm.1), custom_call_target="tpu_custom_call" | custom-call | tf_op jit(solution)/shard_map/moe/pallas_call | solution.py:299
  415.3 2.4 pages.1
  417.7 0.8 copy.55
  (112 shorter events, 20.2 us)
Async XLA Ops:
  7.2 70.5 %copy-start.4 = (f32[128,8]{0,1:T(8,128)S(1)}, f32[128,8]{0,1:T(8,128)}, u32[]{:S(2)}) copy-start(f32[128,8]{0,1:T(8,128)} %param.21) | copy-start | bytes 12292
  7.2 70.6 %copy-start.6 = (s32[128,8]{0,1:T(8,128)S(1)}, s32[128,8]{0,1:T(8,128)}, u32[]{:S(2)}) copy-start(s32[128,8]{0,1:T(8,128)} %param.20) | copy-start | bytes 12292
  7.2 71.2 %copy-start.7 = (s32[1,512]{1,0:T(1,128)S(1)}, s32[1,512]{1,0:T(1,128)}, u32[]{:S(2)}) copy-start(s32[1,512]{1,0:T(1,128)} %param.22) | copy-start | bytes 6148
  7.2 90.9 %all-gather.2.cloned.1.call-start = ((), (), s32[]{:S(2)}) async-start(), calls=%async_computation | async-start | bytes 8519680 | tf_op jit(solution)/shard_map/all_gather | solution.py:550
  98.1 12.4 %copy-start.3 = (s32[1,128]{1,0:T(1,128)S(1)}, s32[1,128]{1,0:T(1,128)}, u32[]{:S(2)}) copy-start(s32[1,128]{1,0:T(1,128)} %param.19) | copy-start | bytes 1540
  110.5 47.8 %copy-start.2 = (bf16[128,2048]{1,0:T(8,128)(2,1)S(1)}, bf16[128,2048]{1,0:T(8,128)(2,1)}, u32[]{:S(2)}) copy-start(bf16[128,2048]{1,0:T(8,128)(2,1)} %param.16) | copy-start | bytes 1572868
  158.4 4.8 %copy-start.5 = (f32[2048]{0:T(1024)S(1)}, f32[2048]{0:T(1024)}, u32[]{:S(2)}) copy-start(f32[2048]{0:T(1024)} %param.24) | copy-start | bytes 24580
  163.1 1.2 copy-start
  415.3 2.4 copy-start.1
Sparse Core Ops, SparseCore 0:
  10.8 87.2 all-gather.1
